TPU v7x, 256 devices: a whole 4x4x8 slice. The times are simulated.
256 devices in a mesh: pix: 16 (over x_hi, z), peak: 16 (over y, x_lo, core).
Axes of the slice: x: 4 (x_hi: 2, x_lo: 2; x = x_hi * 2 + x_lo), y: 4, z: 8, core: 2. Of those that a mesh axis runs over, the one named last changes fastest.
Arguments:
- cube: bfloat16 [65536, 8, 2048], P('pix', None, 'peak'), may hold values from -6 to 6
- pix_factor: bfloat16 [65536, 64], P(('pix', 'peak')), may hold values from -0.8984375 to 0.8984375
- sec_factor: bfloat16 [8, 64], replicated, may hold values from -5 to 5
- peak_factor: bfloat16 [2048, 64], P('peak'), may hold values from -0.046875 to 0.046875
Outputs:
- grad_pix: float32 [65536, 64], P(('pix', 'peak'))
- grad_peak: float32 [2048, 64], P('peak')
All inputs are finite; a program needn't handle non-finite values.
Results may differ from a plain program's by a relative error of at most 0.0003.
Values may be sent and summed in bfloat16 or wider, within the bound.
No kernel may reach another device: no remote copies, remote signals or barrier semaphores. Data moves between devices by JAX's collectives and lax.ppermute only.
A program may use at most 64 MiB of HBM per device.

v0:
```python
import math
import jax
import jax.numpy as jnp
from jax import lax
from jax.sharding import PartitionSpec as P


def on_device(cube, pix_factor, sec_factor, peak_factor):
    pixels = cube.shape[0]
    sections = cube.shape[1]
    peaks = cube.shape[2]
    rank = peak_factor.shape[1]
    fb = sec_factor.astype(jnp.float32)
    fa_own = pix_factor.astype(jnp.float32)
    fc_own = peak_factor.astype(jnp.float32)
    gathered = lax.all_gather(pix_factor, "peak", axis=0, tiled=True)
    ttm = jnp.dot(
        cube.reshape(pixels * sections, peaks), peak_factor, preferred_element_type=jnp.float32
    )
    ttm = ttm.reshape(pixels, sections, rank)
    summed_pix = lax.psum_scatter(
        jnp.sum(ttm * fb[None, :, :], axis=1), "peak", scatter_dimension=0, tiled=True
    )
    partial_peak = jnp.zeros((peaks, rank), jnp.float32)
    for index in range(sections):
        inner = lax.dot_general(
            cube[:, index, :],
            gathered,
            (((0,), (0,)), ((), ())),
            preferred_element_type=jnp.float32,
        )
        partial_peak = partial_peak + inner * fb[index][None, :]
    local_a = jnp.dot(pix_factor.T, pix_factor, preferred_element_type=jnp.float32)
    local_c = jnp.dot(peak_factor.T, peak_factor, preferred_element_type=jnp.float32)
    gram_b = jnp.dot(sec_factor.T, sec_factor, preferred_element_type=jnp.float32)
    gram_a = lax.psum(local_a, ("pix", "peak"))
    gram_c = lax.psum(local_c, "peak")
    grad_pix = summed_pix - jnp.dot(fa_own, gram_b * gram_c, precision=lax.Precision.HIGHEST)
    scale = 1.0 / math.sqrt(float(sections * pixels * lax.axis_size("pix")))
    weight_c = gram_a * gram_b
    total = lax.psum(partial_peak, "pix")
    grad_peak = (total - jnp.dot(fc_own, weight_c, precision=lax.Precision.HIGHEST)) * scale
    return (grad_pix, grad_peak)


def solution(mesh):
    in_specs = (P("pix", None, "peak"), P(("pix", "peak"), None), P(), P("peak", None))
    out_specs = (P(("pix", "peak"), None), P("peak", None))
    return jax.shard_map(
        on_device, mesh=mesh, in_specs=in_specs, out_specs=out_specs, check_vma=False
    )
```

profile of v0, /device:TPU:4, one launch (start us, length us, event | category | flops | bytes accessed | tf_op | source)
XLA Modules:
  0.0 273.6 jit_solution(18076057092134265733)
XLA Ops:
  7.2 0.0 copy-start
  7.2 0.0 reduce-scatter.2.cloned.1.call-start
  7.2 0.7 convert_element_type.2
  7.9 7.9 %multiply_reduce_fusion = f32[4096,64]{0,1:T(8,128)} fusion(f32[8,64]{1,0:T(8,128)S(1)} %convert_element_type.2, bf16[128,64]{0,1:T(8,128)(2,1)S(1)} %copy-done, bf16[4096,8,128]{2,1,0:T(8,128)(2,1)} %param.4), kind=kOutput, calls=%fused_computation | convolution fusion | flops 540803072 | bytes 9455616 | tf_op jit(solution)/shard_map/dot_general | solution.py:17
  15.9 0.0 reduce-scatter.2.cloned.1.call-update
  15.9 0.0 copy-start.1
  15.9 7.7 %copy.7 = bf16[4096,8,128]{2,0,1:T(8,128)(2,1)} copy(bf16[4096,8,128]{2,1,0:T(8,128)(2,1)} %param.4) | data formatting | bytes 16777216 | tf_op args[0]
  23.6 23.0 %all_gather.3 = bf16[4096,64]{0,1:T(8,128)(2,1)S(1)} all-gather(bf16[256,64]{0,1:T(8,128)(2,1)S(1)} %copy-done.1), channel_id=1, replica_groups=mesh['pix'=16,'peak'=16] {'peak'}, dimensions={0}, use_global_device_ids=true | all-gather | bytes 557056 | tf_op jit(solution)/shard_map/all_gather | solution.py:16
  46.6 0.1 fusion.16
  46.7 0.1 fusion.15
  46.8 1.6 convolution_multiply_fusion.7
  48.4 1.5 fusion.7
  50.0 77.0 %psum.23 = f32[64,64]{1,0:T(8,128)S(1)} all-reduce(f32[64,64]{1,0:T(8,128)S(1)} %fusion.16), channel_id=1, replica_groups=mesh['pix'=16,'peak'=16] {'pix','peak'}, use_global_device_ids=true, to_apply=%region_4.0 | all-reduce | flops 4096 | bytes 32768 | tf_op jit(solution)/shard_map/psum | solution.py:36
  126.9 53.7 %psum.21 = f32[64,64]{1,0:T(8,128)S(1)} all-reduce(f32[64,64]{1,0:T(8,128)S(1)} %fusion.15), channel_id=1, replica_groups=mesh['pix'=16,'peak'=16] {'peak'}, use_global_device_ids=true, to_apply=%region_2.0 | all-reduce | flops 4096 | bytes 32768 | tf_op jit(solution)/shard_map/psum | solution.py:37
  180.6 1.5 fusion.6
  182.2 1.5 fusion.5
  183.7 1.5 fusion.4
  185.3 1.5 fusion.3
  186.8 1.5 fusion.2
  188.3 1.5 fusion.1
  189.9 74.1 %psum.22 = f32[128,64]{0,1:T(8,128)S(1)} all-reduce(f32[128,64]{0,1:T(8,128)S(1)} %fusion.1), channel_id=1, replica_groups=mesh['pix'=16,'peak'=16] {'pix'}, use_global_device_ids=true, to_apply=%region_3.0 | all-reduce | flops 8192 | bytes 65536 | tf_op jit(solution)/shard_map/psum | solution.py:41
  264.0 0.2 fusion.14
  264.2 0.8 fusion.9
  265.1 1.7 fusion
  (6 shorter events, 0.0 us)
Async XLA Ops:
  7.2 0.8 copy-start
  7.2 257.9 %reduce-scatter.2.cloned.1.call-start = ((), (), s32[]{:S(2)}) async-start(), calls=%async_computation.1 | async-start | bytes 1114112 | tf_op jit(solution)/shard_map/reduce_scatter | solution.py:21
  15.9 7.7 %copy-start.1 = (bf16[256,64]{0,1:T(8,128)(2,1)S(1)}, bf16[256,64]{0,1:T(8,128)(2,1)}, u32[]{:S(2)}) copy-start(bf16[256,64]{0,1:T(8,128)(2,1)} %param.5) | copy-start | bytes 98308
  23.6 240.4 %copy-start.2 = (bf16[8,64]{1,0:T(8,128)(2,1)S(1)}, bf16[8,64]{1,0:T(8,128)(2,1)}, u32[]{:S(2)}) copy-start(bf16[8,64]{1,0:T(8,128)(2,1)} %param.6) | copy-start | bytes 3076
Sparse Core Ops, SparseCore 0:
  16.0 66.9 reduce-scatter.1
where the time goes:
time: 274 us
  blocking collectives  228 us (83%)
  matrix products  23.3 us (9%)
  between operations  14.1 us (5%)
  local copies, waits for them, and re-layouts  7.72 us (3%)
    psum x1, blocking collectives, on_device(): gram_a = lax.psum(local_a, ('pix', 'peak'))  77 us
    psum x1, blocking collectives, on_device(): total = lax.psum(partial_peak, 'pix')  74.1 us
    psum x1, blocking collectives, on_device(): gram_c = lax.psum(local_c, 'peak')  53.7 us
    all_gather x1, blocking collectives, on_device(): gathered = lax.all_gather(pix_factor, 'peak', axis=0, tiled=True)  23 us
    dot_general x8, matrix products, on_device(): lax.dot_general(cube[:, index, :], gathered, (((0,), (0,)), ((), ())), pr...  12.4 us
    dot_general x1, matrix products, on_device(): jnp.dot(cube.reshape(pixels * sections, peaks), peak_factor, preferred_el...  7.95 us
    unnamed x7, local copies, waits for them, and re-layouts  7.71 us
  transfers between devices with their start and end apart: 1, of which 0 were waited for; matrix products, arithmetic and copies ran while one was open for 8% of the time, Pallas kernels for 0%

commit v1 on v0

--- a/solution.py
+++ b/solution.py
@@ -33,7 +33,9 @@
     local_a = jnp.dot(pix_factor.T, pix_factor, preferred_element_type=jnp.float32)
     local_c = jnp.dot(peak_factor.T, peak_factor, preferred_element_type=jnp.float32)
     gram_b = jnp.dot(sec_factor.T, sec_factor, preferred_element_type=jnp.float32)
-    gram_a = lax.psum(local_a, ("pix", "peak"))
+    gram_a = local_a
+    for dd in ("peak", "pix"):
+        gram_a = lax.psum(gram_a, axis_name=dd)
     gram_c = lax.psum(local_c, "peak")
     grad_pix = summed_pix - jnp.dot(fa_own, gram_b * gram_c, precision=lax.Precision.HIGHEST)
     scale = 1.0 / math.sqrt(float(sections * pixels * lax.axis_size("pix")))

time: 274 us -> 200 us (0.73)
  blocking collectives: 228 us -> 153 us
    psum x1 -> x0, blocking collectives: 77 us -> none  [on_device(): gram_a = lax.psum(local_a, ('pix', 'peak'))]
    psum x1, blocking collectives: 74.1 us -> 76.9 us  [on_device(): total = lax.psum(partial_peak, 'pix')]
  transfers between devices with their start and end apart: 1 -> 1, of which waited for: 0 -> 0; matrix products, arithmetic and copies ran while one was open for 8% -> 11% of each run, Pallas kernels for 0% -> 0%
where the time goes in v1:
time: 200 us; the launch traced here: 199 us
  blocking collectives  153 us (76%)
  matrix products  23.3 us (12%)
  between operations  14.1 us (7%)
  local copies, waits for them, and re-layouts  7.72 us (4%)
    psum x1, blocking collectives, on_device(): total = lax.psum(partial_peak, 'pix')  76.9 us
    psum x1, blocking collectives, on_device(): gram_c = lax.psum(local_c, 'peak')  53.2 us
    all_gather x1, blocking collectives, on_device(): gathered = lax.all_gather(pix_factor, 'peak', axis=0, tiled=True)  23 us
    dot_general x8, matrix products, on_device(): lax.dot_general(cube[:, index, :], gathered, (((0,), (0,)), ((), ())), pr...  12.3 us
    dot_general x1, matrix products, on_device(): jnp.dot(cube.reshape(pixels * sections, peaks), peak_factor, preferred_el...  7.95 us
    unnamed x7, local copies, waits for them, and re-layouts  7.71 us
  transfers between devices with their start and end apart: 1, of which 0 were waited for; matrix products, arithmetic and copies ran while one was open for 11% of the time, Pallas kernels for 0%

profile of v1, /device:TPU:4, one launch (start us, length us, event | category | flops | bytes accessed | tf_op | source)
XLA Modules:
  0.0 199.0 jit_solution(11312229132398940934)
XLA Ops:
  7.2 0.0 copy-start
  7.2 0.0 reduce-scatter.2.cloned.1.call-start
  7.2 0.7 convert_element_type.2
  7.9 0.0 copy-done
  7.9 7.9 %multiply_reduce_fusion = f32[4096,64]{0,1:T(8,128)} fusion(f32[8,64]{1,0:T(8,128)S(1)} %convert_element_type.2, bf16[128,64]{0,1:T(8,128)(2,1)S(1)} %copy-done, bf16[4096,8,128]{2,1,0:T(8,128)(2,1)} %param.4), kind=kOutput, calls=%fused_computation | convolution fusion | flops 540803072 | bytes 9455616 | tf_op jit(solution)/shard_map/dot_general | solution.py:17
  15.9 0.0 reduce-scatter.2.cloned.1.call-update
  15.9 0.0 copy-start.1
  15.9 7.7 %copy.7 = bf16[4096,8,128]{2,0,1:T(8,128)(2,1)} copy(bf16[4096,8,128]{2,1,0:T(8,128)(2,1)} %param.4) | data formatting | bytes 16777216 | tf_op args[0]
  23.6 23.0 %all_gather.3 = bf16[4096,64]{0,1:T(8,128)(2,1)S(1)} all-gather(bf16[256,64]{0,1:T(8,128)(2,1)S(1)} %copy-done.1), channel_id=1, replica_groups=mesh['pix'=16,'peak'=16] {'peak'}, dimensions={0}, use_global_device_ids=true | all-gather | bytes 557056 | tf_op jit(solution)/shard_map/all_gather | solution.py:16
  46.6 0.1 fusion.16
  46.7 1.6 convolution_multiply_fusion.7
  48.3 1.5 fusion.7
  49.8 0.1 fusion.15
  49.9 53.2 %all-reduce = (f32[64,64]{1,0:T(8,128)S(1)}, f32[64,64]{1,0:T(8,128)S(1)}) all-reduce(f32[64,64]{1,0:T(8,128)S(1)} %fusion.15, f32[64,64]{1,0:T(8,128)S(1)} %fusion.16), channel_id=1, replica_groups=mesh['pix'=16,'peak'=16] {'peak'}, use_global_device_ids=true, to_apply=%region_2.0 | all-reduce | flops 8192 | bytes 65536 | tf_op jit(solution)/shard_map/psum | solution.py:39
  103.2 1.5 fusion.6
  104.7 1.5 fusion.5
  106.3 1.5 fusion.4
  107.8 1.5 fusion.3
  109.4 1.5 fusion.2
  110.9 1.5 fusion.1
  112.5 76.9 %all-reduce.1 = (f32[128,64]{0,1:T(8,128)S(1)}, f32[64,64]{1,0:T(8,128)S(1)}) all-reduce(f32[128,64]{0,1:T(8,128)S(1)} %fusion.1, f32[64,64]{1,0:T(8,128)S(1)} %get-tuple-element.3), channel_id=1, replica_groups=mesh['pix'=16,'peak'=16] {'pix'}, use_global_device_ids=true, to_apply=%region_3.0 | all-reduce | flops 12288 | bytes 98304 | tf_op jit(solution)/shard_map/psum | solution.py:43
  189.4 0.2 fusion.14
  189.6 0.8 fusion.9
  190.4 1.7 fusion
  (5 shorter events, 0.0 us)
Async XLA Ops:
  7.2 0.8 copy-start
  7.2 183.2 %reduce-scatter.2.cloned.1.call-start = ((), (), s32[]{:S(2)}) async-start(), calls=%async_computation.1 | async-start | bytes 1114112 | tf_op jit(solution)/shard_map/reduce_scatter | solution.py:21
  15.9 7.7 %copy-start.1 = (bf16[256,64]{0,1:T(8,128)(2,1)S(1)}, bf16[256,64]{0,1:T(8,128)(2,1)}, u32[]{:S(2)}) copy-start(bf16[256,64]{0,1:T(8,128)(2,1)} %param.5) | copy-start | bytes 98308
  23.6 165.8 %copy-start.2 = (bf16[8,64]{1,0:T(8,128)(2,1)S(1)}, bf16[8,64]{1,0:T(8,128)(2,1)}, u32[]{:S(2)}) copy-start(bf16[8,64]{1,0:T(8,128)(2,1)} %param.6) | copy-start | bytes 3076
Sparse Core Ops, SparseCore 0:
  16.0 66.7 reduce-scatter.1

commit v2 on v0

--- a/solution.py
+++ b/solution.py
@@ -3,6 +3,11 @@
 import jax.numpy as jnp
 from jax import lax
 from jax.sharding import PartitionSpec as P
+from jax.lax import all_gather
+
+
+def tell_counts_all(vector, which_axis):
+    return all_gather(vector, which_axis).sum(axis=0)
 
 
 def on_device(cube, pix_factor, sec_factor, peak_factor):
@@ -34,7 +39,7 @@
     local_c = jnp.dot(peak_factor.T, peak_factor, preferred_element_type=jnp.float32)
     gram_b = jnp.dot(sec_factor.T, sec_factor, preferred_element_type=jnp.float32)
     gram_a = lax.psum(local_a, ("pix", "peak"))
-    gram_c = lax.psum(local_c, "peak")
+    gram_c = tell_counts_all(local_c, "peak")
     grad_pix = summed_pix - jnp.dot(fa_own, gram_b * gram_c, precision=lax.Precision.HIGHEST)
     scale = 1.0 / math.sqrt(float(sections * pixels * lax.axis_size("pix")))
     weight_c = gram_a * gram_b

time: 274 us -> 241 us (0.88)
  blocking collectives: 228 us -> 194 us
    psum x1 -> x0, blocking collectives: 53.7 us -> none  [on_device(): gram_c = lax.psum(local_c, 'peak')]
    all_gather x0 -> x1, blocking collectives: none -> 19.1 us  [tell_counts_all(): return all_gather(vector, which_axis).sum(axis=0)]
  transfers between devices with their start and end apart: 1 -> 1, of which waited for: 0 -> 0; matrix products, arithmetic and copies ran while one was open for 8% -> 9% of each run, Pallas kernels for 0% -> 0%
where the time goes in v2:
time: 241 us; the launch traced here: 240 us
  blocking collectives  194 us (80%)
  matrix products  23.3 us (10%)
  between operations  14.1 us (6%)
  local copies, waits for them, and re-layouts  7.72 us (3%)
    psum x1, blocking collectives, on_device(): gram_a = lax.psum(local_a, ('pix', 'peak'))  76.8 us
    psum x1, blocking collectives, on_device(): total = lax.psum(partial_peak, 'pix')  75 us
    all_gather x1, blocking collectives, on_device(): gathered = lax.all_gather(pix_factor, 'peak', axis=0, tiled=True)  23 us
    all_gather x1, blocking collectives, tell_counts_all(): return all_gather(vector, which_axis).sum(axis=0)  19.1 us
    dot_general x8, matrix products, on_device(): lax.dot_general(cube[:, index, :], gathered, (((0,), (0,)), ((), ())), pr...  12.3 us
    dot_general x1, matrix products, on_device(): jnp.dot(cube.reshape(pixels * sections, peaks), peak_factor, preferred_el...  7.95 us
    unnamed x7, local copies, waits for them, and re-layouts  7.71 us
  transfers between devices with their start and end apart: 1, of which 0 were waited for; matrix products, arithmetic and copies ran while one was open for 9% of the time, Pallas kernels for 0%

profile of v2, /device:TPU:4, one launch (start us, length us, event | category | flops | bytes accessed | tf_op | source)
XLA Modules:
  0.0 239.7 jit_solution(1521257946146376661)
XLA Ops:
  7.2 0.0 copy-start
  7.2 0.0 reduce-scatter.2.cloned.1.call-start
  7.2 0.7 convert_element_type.2
  7.9 7.9 %multiply_reduce_fusion = f32[4096,64]{0,1:T(8,128)} fusion(f32[8,64]{1,0:T(8,128)S(1)} %convert_element_type.2, bf16[128,64]{0,1:T(8,128)(2,1)S(1)} %copy-done, bf16[4096,8,128]{2,1,0:T(8,128)(2,1)} %param.4), kind=kOutput, calls=%fused_computation | convolution fusion | flops 540803072 | bytes 9455616 | tf_op jit(solution)/shard_map/dot_general | solution.py:22
  15.9 0.0 reduce-scatter.2.cloned.1.call-update
  15.9 0.0 copy-start.1
  15.9 7.7 %copy.7 = bf16[4096,8,128]{2,0,1:T(8,128)(2,1)} copy(bf16[4096,8,128]{2,1,0:T(8,128)(2,1)} %param.4) | data formatting | bytes 16777216 | tf_op args[0]
  23.6 23.0 %all_gather.11 = bf16[4096,64]{0,1:T(8,128)(2,1)S(1)} all-gather(bf16[256,64]{0,1:T(8,128)(2,1)S(1)} %copy-done.1), channel_id=1, replica_groups=mesh['pix'=16,'peak'=16] {'peak'}, dimensions={0}, use_global_device_ids=true | all-gather | bytes 557056 | tf_op jit(solution)/shard_map/all_gather | solution.py:21
  46.6 0.1 fusion.16
  46.7 0.1 fusion.15
  46.8 1.6 convolution_multiply_fusion.7
  48.4 1.5 fusion.7
  50.0 19.1 %all-gather = f32[1024,64]{1,0:T(8,128)S(1)} all-gather(f32[64,64]{1,0:T(8,128)S(1)} %fusion.15), channel_id=2, replica_groups=mesh['pix'=16,'peak'=16] {'peak'}, dimensions={0}, use_global_device_ids=true | all-gather | bytes 278528 | tf_op jit(solution)/shard_map/all_gather | solution.py:10
  69.1 76.8 %psum.15 = f32[64,64]{1,0:T(8,128)S(1)} all-reduce(f32[64,64]{1,0:T(8,128)S(1)} %fusion.16), channel_id=1, replica_groups=mesh['pix'=16,'peak'=16] {'pix','peak'}, use_global_device_ids=true, to_apply=%region_4.0 | all-reduce | flops 4096 | bytes 32768 | tf_op jit(solution)/shard_map/psum | solution.py:41
  145.9 1.5 fusion.6
  147.4 1.5 fusion.5
  149.0 1.5 fusion.4
  150.5 1.5 fusion.3
  152.1 1.5 fusion.2
  153.6 1.5 fusion.1
  155.2 75.0 %psum.14 = f32[128,64]{0,1:T(8,128)S(1)} all-reduce(f32[128,64]{0,1:T(8,128)S(1)} %fusion.1), channel_id=1, replica_groups=mesh['pix'=16,'peak'=16] {'pix'}, use_global_device_ids=true, to_apply=%region_3.0 | all-reduce | flops 8192 | bytes 65536 | tf_op jit(solution)/shard_map/psum | solution.py:46
  230.1 0.2 fusion.14
  230.3 0.8 fusion.9
  231.2 1.7 fusion
  (7 shorter events, 0.1 us)
Async XLA Ops:
  7.2 0.8 copy-start
  7.2 224.0 %reduce-scatter.2.cloned.1.call-start = ((), (), s32[]{:S(2)}) async-start(), calls=%async_computation.1 | async-start | bytes 1114112 | tf_op jit(solution)/shard_map/reduce_scatter | solution.py:26
  15.9 7.7 %copy-start.1 = (bf16[256,64]{0,1:T(8,128)(2,1)S(1)}, bf16[256,64]{0,1:T(8,128)(2,1)}, u32[]{:S(2)}) copy-start(bf16[256,64]{0,1:T(8,128)(2,1)} %param.5) | copy-start | bytes 98308
  23.6 206.5 %copy-start.2 = (bf16[8,64]{1,0:T(8,128)(2,1)S(1)}, bf16[8,64]{1,0:T(8,128)(2,1)}, u32[]{:S(2)}) copy-start(bf16[8,64]{1,0:T(8,128)(2,1)} %param.6) | copy-start | bytes 3076
Sparse Core Ops, SparseCore 0:
  16.0 66.9 reduce-scatter.1
